TPU v7x, 256 devices: a whole 4x4x8 slice. The times are simulated.
256 devices in a mesh: dp: 2 (over core), ctx: 32 (over z, y), head: 4 (over x).
Axes of the slice: x: 4, y: 4, z: 8, core: 2. Of those that a mesh axis runs over, the one named last changes fastest.
Arguments:
- x_raw: bfloat16 [2, 8192, 8192], P('dp', 'ctx', 'head'), may hold values from -6 to 6
- bc_raw: bfloat16 [2, 8192, 2, 1024], P('dp', 'ctx', None, 'head'), may hold values from -6 to 6
- z_gate: bfloat16 [2, 8192, 8192], P('dp', 'ctx', 'head'), may hold values from -20 to 20
- dt_raw: bfloat16 [2, 128, 8192], P('dp', 'head', 'ctx'), may hold values from -4 to 4
- resets: int32 [2, 8192], P('dp', 'ctx'), may hold values 0 or 1
- conv_x_weight: float32 [4, 8192], P(None, 'head'), may hold values from -3 to 3
- conv_x_bias: float32 [8192], P('head'), may hold values from -1.5 to 1.5
- conv_bc_weight: float32 [4, 2, 1024], P(None, None, 'head'), may hold values from -3 to 3
- conv_bc_bias: float32 [2, 1024], P(None, 'head'), may hold values from -1.5 to 1.5
- a_log: float32 [128], P('head'), may hold values from -9 to 1
- dt_bias: float32 [128], P('head'), may hold values from -13 to -3
- skip_weight: float32 [128], P('head'), may hold values from 0.5 to 2
- norm_gain: float32 [8192], P('head'), may hold values from 0.1 to 1.9
- grad_out: bfloat16 [2, 8192, 8192], P('dp', 'ctx', 'head'), may hold values from -6 to 6
Outputs:
- grad_x: bfloat16 [2, 8192, 8192], P('dp', 'ctx', 'head')
- grad_bc: bfloat16 [2, 8192, 2, 1024], P('dp', 'ctx', None, 'head')
- grad_z: bfloat16 [2, 8192, 8192], P('dp', 'ctx', 'head')
- grad_dt: float32 [2, 128, 8192], P('dp', 'head', 'ctx')
- grad_conv_x_weight: float32 [4, 8192], P(None, 'head')
- grad_conv_x_bias: float32 [8192], P('head')
- grad_conv_bc_weight: float32 [4, 2, 1024], P(None, None, 'head')
- grad_conv_bc_bias: float32 [2, 1024], P(None, 'head')
- grad_a_log: float32 [128], P('head')
- grad_dt_bias: float32 [128], P('head')
- grad_skip: float32 [128], P('head')
- grad_gain: float32 [8192], P('head')
All inputs are finite; a program needn't handle non-finite values. No bound on the sum of `resets` on one device may be relied on, other than what follows from the above.
Results may differ from a plain program's by a relative error of at most 0.01595.
Values may be sent and summed in bfloat16 or wider, within the bound.
A program may use at most 256 MiB of HBM per device.

v0:
```python
import functools
import jax
import jax.numpy as jnp
from jax import lax
from jax.sharding import PartitionSpec as P

HEAD_DIM = 64
NSTATE = 128
CONV = 4
STRETCH = 128
INNER = 8192
norm_eps = 1e-05


def from_behind(value, axis, steps):
    count = lax.axis_size(axis)
    first, last = (max(0, -steps), min(count, count - steps))
    return lax.ppermute(value, axis, [(source, source + steps) for source in range(first, last)])


def entering(value, axis, join, neutral, backward):
    count, mine = (lax.axis_size(axis), lax.axis_index(axis))
    pieces = jax.tree.map(lambda part: lax.all_gather(part, axis), value)
    if backward:
        pieces = jax.tree.map(lambda part: part[::-1], pieces)
        mine = count - 1 - mine
    running = jax.tree.map(
        lambda part, zero: jnp.full_like(part, 0) + jnp.asarray(zero, part.dtype), value, neutral
    )

    def step(position, running):
        longer = join(running, jax.tree.map(lambda part: part[position], pieces))
        return jax.tree.map(lambda new, old: jnp.where(position < mine, new, old), longer, running)

    return lax.fori_loop(0, count - 1, step, running)


def kept(value):
    return lax.optimization_barrier(value)


def causal_conv(extended, counts, weight, conv_bias):
    pad_rows = CONV - 1
    row_count = extended.shape[0] - pad_rows
    shape_tail = (1,) * (extended.ndim - 1)
    summed = conv_bias + weight[0] * extended[pad_rows:]
    for lag_step in range(1, CONV):
        lower = pad_rows - lag_step
        live_mask = (counts[pad_rows:] == counts[lower : lower + row_count]).astype(jnp.float32)
        summed = summed + weight[lag_step] * extended[
            lower : lower + row_count
        ] * live_mask.reshape((row_count,) + shape_tail)
    return kept(jax.nn.silu(summed).astype(jnp.bfloat16))


def rows_to_blocks(array_rows):
    return array_rows.reshape((array_rows.shape[0] // STRETCH, STRETCH) + array_rows.shape[1:])


def steps_to_blocks(steps_dt):
    shape_now = steps_dt.shape
    reshaped = steps_dt.reshape(shape_now[0], shape_now[1], shape_now[2] // STRETCH, STRETCH)
    return jnp.transpose(reshaped, (2, 0, 1, 3))


def from_before(block_c, prior_state, running, resets_seen):
    from_start = jnp.where(resets_seen == 0.0, jnp.exp(running), 0.0)
    state_half = prior_state.astype(jnp.bfloat16)
    carried = jnp.einsum("tgn,ghpn->tghp", block_c, state_half, preferred_element_type=jnp.float32)
    return carried * jnp.transpose(from_start, (2, 0, 1))[..., None]


def keep_factor(running, resets_seen):
    return jnp.where(resets_seen[-1] == 0.0, jnp.exp(running[..., -1]), 0.0)


def block_end(block_x, block_b, block_dt, running, resets_seen):
    to_end = jnp.where(resets_seen == resets_seen[-1], jnp.exp(running[..., -1:] - running), 0.0)
    scaled = (
        block_x.astype(jnp.float32) * jnp.transpose(block_dt * to_end, (2, 0, 1))[..., None]
    ).astype(jnp.bfloat16)
    return jnp.einsum("sghp,sgn->ghpn", scaled, block_b, preferred_element_type=jnp.float32)


def block_terms(prior_state, block_piece, decay_rate):
    block_x, block_b, block_c, block_dt, block_flags = block_piece
    running = jnp.cumsum(-decay_rate[:, :, None] * block_dt, axis=-1)
    resets_seen = jnp.cumsum(block_flags)
    position = jnp.arange(block_flags.shape[0])
    same_doc = (resets_seen[:, None] == resets_seen[None, :]) & (
        position[:, None] >= position[None, :]
    )
    spread = running[..., :, None] - running[..., None, :]
    segment = jnp.where(same_doc, jnp.exp(jnp.where(same_doc, spread, 0.0)), 0.0)
    scores = jnp.einsum("tgn,sgn->gts", block_c, block_b, preferred_element_type=jnp.float32)
    weights = (scores[:, None] * segment * block_dt[:, :, None, :]).astype(jnp.bfloat16)
    within = jnp.einsum("ghts,sghp->tghp", weights, block_x, preferred_element_type=jnp.float32)
    carried = from_before(block_c, prior_state, running, resets_seen)
    fresh_state = block_end(block_x, block_b, block_dt, running, resets_seen)
    next_state = keep_factor(running, resets_seen)[..., None, None] * prior_state + fresh_state
    return (next_state, within + carried)


def scan_blocks(inputs, b_rows, c_rows, steps_dt, decay_rate, reset_flags, state_in):
    row_count = inputs.shape[0]
    pieces = (
        rows_to_blocks(inputs),
        rows_to_blocks(b_rows),
        rows_to_blocks(c_rows),
        steps_to_blocks(steps_dt),
        rows_to_blocks(reset_flags),
    )
    stepper = functools.partial(block_terms, decay_rate=decay_rate)
    final_state, outputs = lax.scan(stepper, state_in, pieces)
    return (outputs.reshape((row_count,) + inputs.shape[1:]), final_state)


def block_ends(inputs, b_rows, steps_dt, decay_rate, reset_flags):

    def block_advance(carried_pair, block_piece):
        product, prior_state = carried_pair
        part_x, part_b, part_dt, part_flags = block_piece
        running = jnp.cumsum(-decay_rate[:, :, None] * part_dt, axis=-1)
        resets_seen = jnp.cumsum(part_flags)
        keep_all = keep_factor(running, resets_seen)
        fresh_state = block_end(part_x, part_b, part_dt, running, resets_seen)
        return ((product * keep_all, keep_all[..., None, None] * prior_state + fresh_state), None)

    start_pair = (
        jnp.ones(decay_rate.shape, jnp.float32),
        jnp.zeros(decay_rate.shape + (HEAD_DIM, NSTATE), jnp.float32),
    )
    pieces = (
        rows_to_blocks(inputs),
        rows_to_blocks(b_rows),
        steps_to_blocks(steps_dt),
        rows_to_blocks(reset_flags),
    )
    end_pair, unused = lax.scan(block_advance, start_pair, pieces)
    return end_pair


def carried_only(c_rows, steps_dt, decay_rate, reset_flags, prior_state):

    def carried_advance(state_now, block_piece):
        part_c, part_dt, part_flags = block_piece
        running = jnp.cumsum(-decay_rate[:, :, None] * part_dt, axis=-1)
        resets_seen = jnp.cumsum(part_flags)
        carried = from_before(part_c, state_now, running, resets_seen)
        return (keep_factor(running, resets_seen)[..., None, None] * state_now, carried)

    pieces = (rows_to_blocks(c_rows), steps_to_blocks(steps_dt), rows_to_blocks(reset_flags))
    final_state, outputs = lax.scan(carried_advance, prior_state, pieces)
    return outputs.reshape((c_rows.shape[0], c_rows.shape[1], steps_dt.shape[1], HEAD_DIM))


def gate_output(y_ssd, inputs, z_in, skip_weight):
    row_count = inputs.shape[0]
    skip_term = skip_weight.reshape(inputs.shape[1], inputs.shape[2])[
        None, :, :, None
    ] * inputs.astype(jnp.float32)
    mixed = kept((y_ssd + skip_term).astype(jnp.bfloat16))
    return mixed.astype(jnp.float32).reshape(row_count, -1) * jax.nn.silu(z_in)


def combine_pairs(earlier, later):
    return (earlier[0] * later[0], later[0][..., None, None] * earlier[1] + later[1])


def per_device(
    x_raw,
    bc_raw,
    z_gate,
    dt_raw,
    resets,
    conv_x_weight,
    conv_x_bias,
    conv_bc_weight,
    conv_bc_bias,
    a_log,
    dt_bias,
    skip_weight,
    norm_gain,
    grad_out,
):
    halo_rows = CONV - 1
    row_count = x_raw.shape[1]
    g_count = bc_raw.shape[3] // NSTATE
    heads_dev = a_log.shape[0]
    per_group = heads_dev // g_count
    reset_flags = resets[0].astype(jnp.float32)
    counts = jnp.cumsum(reset_flags)
    tail_keep = (counts[-halo_rows:] == counts[-1]).astype(jnp.float32)
    tail_half = tail_keep.astype(jnp.bfloat16)
    x_own = x_raw[0]
    bc_own = bc_raw[0]
    x_prev, bc_prev = from_behind(
        (x_own[-halo_rows:] * tail_half[:, None], bc_own[-halo_rows:] * tail_half[:, None, None]),
        "ctx",
        1,
    )
    x_ext = jnp.concatenate([x_prev, x_own]).astype(jnp.float32)
    bc_ext = jnp.concatenate([bc_prev, bc_own]).astype(jnp.float32)
    padded_counts = jnp.concatenate([jnp.zeros((halo_rows,), jnp.float32), counts])
    z_in = z_gate[0].astype(jnp.float32)
    dt_in = dt_raw[0].astype(jnp.float32)

    def conv_part(x_wide, bc_wide, dt_values, cx_weight, cx_bias, cb_weight, cb_bias, bias_dt):
        inputs = causal_conv(x_wide, padded_counts, cx_weight, cx_bias).reshape(
            row_count, g_count, per_group, HEAD_DIM
        )
        bc_conv = causal_conv(bc_wide, padded_counts, cb_weight, cb_bias)
        b_rows = bc_conv[:, 0].reshape(row_count, g_count, NSTATE)
        c_rows = bc_conv[:, 1].reshape(row_count, g_count, NSTATE)
        steps_dt = jax.nn.softplus(dt_values + bias_dt[:, None]).reshape(
            g_count, per_group, row_count
        )
        return (inputs, b_rows, c_rows, steps_dt)

    conv_outs, conv_pull = jax.vjp(
        conv_part,
        x_ext,
        bc_ext,
        dt_in,
        conv_x_weight,
        conv_x_bias,
        conv_bc_weight,
        conv_bc_bias,
        dt_bias,
    )
    inputs, b_rows, c_rows, steps_dt = conv_outs
    decay_rate = jnp.exp(a_log).reshape(g_count, per_group)
    device_decay, device_state = block_ends(inputs, b_rows, steps_dt, decay_rate, reset_flags)
    unit_decay = jnp.ones_like(device_decay)
    prefix_pair = entering(
        (device_decay, device_state),
        "ctx",
        combine_pairs,
        (unit_decay, jnp.zeros_like(device_state)),
        False,
    )
    state_in = prefix_pair[1]

    def ssd_part(block_inputs, block_b, block_c, block_dt, log_rate, prior_state):
        rate_now = jnp.exp(log_rate).reshape(g_count, per_group)
        return scan_blocks(
            block_inputs, block_b, block_c, block_dt, rate_now, reset_flags, prior_state
        )

    ssd_outs, ssd_pull = jax.vjp(ssd_part, inputs, b_rows, c_rows, steps_dt, a_log, state_in)
    y_ssd = ssd_outs[0]
    gated, post_pull = jax.vjp(gate_output, y_ssd, inputs, z_in, skip_weight)
    cotangent = grad_out[0].astype(jnp.float32)
    gained_out = cotangent * norm_gain
    row_totals = lax.psum(
        (jnp.sum(gated * gated, axis=-1), jnp.sum(gated * gained_out, axis=-1)), "head"
    )
    inv_rms = lax.rsqrt(row_totals[0] / INNER + norm_eps)
    d_gated = (
        gained_out * inv_rms[:, None]
        - gated * (inv_rms * inv_rms * inv_rms * row_totals[1] / INNER)[:, None]
    )
    gain_local = jnp.sum(cotangent * gated * inv_rms[:, None], axis=0)
    dy_ssd, d_inputs_post, d_z, d_skip = post_pull(d_gated)
    carried_map = functools.partial(carried_only, c_rows, steps_dt, decay_rate, reset_flags)
    unused_out, carried_pull = jax.vjp(carried_map, state_in)
    direct_adjoint = carried_pull(dy_ssd)[0]
    later_pair = entering(
        (device_decay, direct_adjoint),
        "ctx",
        combine_pairs,
        (unit_decay, jnp.zeros_like(direct_adjoint)),
        True,
    )
    d_inputs, d_b, d_c, d_dt, d_alog, d_state = ssd_pull((dy_ssd, later_pair[1]))
    d_inputs = d_inputs + d_inputs_post
    d_x_ext, d_bc_ext, d_dt_in, d_cxw, d_cxb, d_cbw, d_cbb, d_dt_bias = conv_pull(
        (d_inputs, d_b, d_c, d_dt)
    )
    back_x, back_bc = from_behind((d_x_ext[:halo_rows], d_bc_ext[:halo_rows]), "ctx", -1)
    grad_x_rows = jnp.concatenate(
        [d_x_ext[halo_rows:row_count], d_x_ext[row_count:] + back_x * tail_keep[:, None]]
    )
    grad_bc_rows = jnp.concatenate(
        [d_bc_ext[halo_rows:row_count], d_bc_ext[row_count:] + back_bc * tail_keep[:, None, None]]
    )
    local_terms = (d_cxw, d_cxb, d_cbw, d_cbb, d_alog, d_dt_bias, d_skip, gain_local)
    summed_terms = lax.psum(
        (
            local_terms[0],
            local_terms[1],
            local_terms[2],
            local_terms[3],
            local_terms[4],
            local_terms[5],
            local_terms[6],
            local_terms[7],
        ),
        ("dp", "ctx"),
    )
    grad_scale = float(lax.axis_size("dp") * lax.axis_size("ctx") * row_count) ** (-0.5)
    return (
        grad_x_rows[None].astype(jnp.bfloat16),
        grad_bc_rows[None].astype(jnp.bfloat16),
        d_z[None].astype(jnp.bfloat16),
        d_dt_in[None],
        summed_terms[0] * grad_scale,
        summed_terms[1] * grad_scale,
        summed_terms[2] * grad_scale,
        summed_terms[3] * grad_scale,
        summed_terms[4] * grad_scale,
        summed_terms[5] * grad_scale,
        summed_terms[6] * grad_scale,
        summed_terms[7] * grad_scale,
    )


def solution(mesh):
    return jax.shard_map(
        per_device,
        mesh=mesh,
        in_specs=(
            P("dp", "ctx", "head"),
            P("dp", "ctx", None, "head"),
            P("dp", "ctx", "head"),
            P("dp", "head", "ctx"),
            P("dp", "ctx"),
            P(None, "head"),
            P("head"),
            P(None, None, "head"),
            P(None, "head"),
            P("head"),
            P("head"),
            P("head"),
            P("head"),
            P("dp", "ctx", "head"),
        ),
        out_specs=(
            P("dp", "ctx", "head"),
            P("dp", "ctx", None, "head"),
            P("dp", "ctx", "head"),
            P("dp", "head", "ctx"),
            P(None, "head"),
            P("head"),
            P(None, None, "head"),
            P(None, "head"),
            P("head"),
            P("head"),
            P("head"),
            P("head"),
        ),
        check_vma=False,
    )
```

profile of v0, /device:TPU:128, one launch (start us, length us, event | category | flops | bytes accessed | tf_op | source)
XLA Modules:
  0.0 1191.2 jit_solution(14840181272702812922)
XLA Ops:
  12.5 3.5 collective-permute-start
  17.0 3.5 collective-permute-start.1
  30.2 3.7 multiply_convert_fusion.7
  34.9 3.1 reshape.652
  38.1 3.3 copy.180
  41.4 11.3 while.160
  61.7 10.0 while.158
  74.3 41.9 %all-gather.3 = f32[32,2,16]{2,1,0:T(2,128)S(1)} all-gather(f32[1,2,16]{2,1,0:T(2,128)S(1)} %bitcast.631), channel_id=2, replica_groups=mesh['dp'=2,'ctx'=32,'head'=4] {'ctx'}, dimensions={0}, use_global_device_ids=true | all-gather | bytes 4224 | tf_op jit(solution)/shard_map/all_gather | solution.py:23
  116.3 168.9 %all-gather.7.cloned.1.call-done = f32[64,16,64,128]{3,2,1,0:T(8,128)} async-done(((f32[2,16,64,128]{3,2,1,0:T(8,128)}), f32[64,16,64,128]{3,2,1,0:T(8,128)}) %all-gather.7.cloned.1.call-update) | async-done | bytes 33554448 | tf_op jit(solution)/shard_map/all_gather | solution.py:23
  285.2 46.6 %while.161 = (s32[]{:T(128)}, f32[2,16,64,128]{3,2,1,0:T(8,128)S(1)}, s32[]{:T(128)}, f32[32,2,16]{2,1,0:T(2,128)S(1)}, f32[32,2,16,64,128]{4,3,2,1,0:T(8,128)}, /*index=5*/s32[]{:T(128)}, s32[]{:T(128)}) while((s32[]{:T(128)}, f32[2,16,64,128]{3,2,1,0:T(8,128)S(1)}, s32[]{:T(128)}, f32[32,2,16]{2,1,0:T(2,128)S(1)}, ...), condition=%wide.region_7.8_spmd.clone, body=%wide.region_6.7_spmd.clone.sunk | while | flops 1048580 | bytes 3146225 | solution.py:35
  334.8 110.5 %while.159 = (s32[]{:T(128)}, f32[2,16,64,128]{3,2,1,0:T(8,128)S(1)}, f32[2,128,2,16,64]{1,0,4,3,2:T(2,128)}, pred[2,2,16,128,128]{4,3,2,1,0:T(32,128)(4,1)}, f3...) while((s32[]{:T(128)}, ...), condition=%wide.region_11.12_spmd.clone, body=%wide.region_8.11_spmd.clone.sunk | while | flops 222142656 | bytes 67194320 | solution.py:114
  350.2 25.0 %dynamic_update_slice.324 = f32[2,128,2,16,64]{1,0,4,3,2:T(2,128)} dynamic-update-slice(f32[2,128,2,16,64]{1,0,4,3,2:T(2,128)} %get-tuple-element.3483, f32[1,128,2,16,64]{1,0,4,3,2:T(1,128)} %bitcast.609, s32[]{:T(128)S(6)} %copy.383, s32[]{:T(128)} %constant.352.clone.1..sunk, s32[]{:T(128)} %constant.352.clone.1..sunk, s32[]{:T(128)} %constant.352.clone.1..sunk, s32[]{:T(128)} %constant.352.clone.1..sunk) | dynamic-update-slice | bytes 2097156 | tf_op jit(solution)/shard_map/jvp()/while/body/jit(dynamic_update_index_in_dim)/dynamic_update_slice | solution.py:114
  376.9 4.0 fusion.249
  405.4 25.0 %dynamic_update_slice.324 = f32[2,128,2,16,64]{1,0,4,3,2:T(2,128)} dynamic-update-slice(f32[2,128,2,16,64]{1,0,4,3,2:T(2,128)} %get-tuple-element.3483, f32[1,128,2,16,64]{1,0,4,3,2:T(1,128)} %bitcast.609, s32[]{:T(128)S(6)} %copy.383, s32[]{:T(128)} %constant.352.clone.1..sunk, s32[]{:T(128)} %constant.352.clone.1..sunk, s32[]{:T(128)} %constant.352.clone.1..sunk, s32[]{:T(128)} %constant.352.clone.1..sunk) | dynamic-update-slice | bytes 2097156 | tf_op jit(solution)/shard_map/jvp()/while/body/jit(dynamic_update_index_in_dim)/dynamic_update_slice | solution.py:114
  432.2 4.0 fusion.249
  445.3 4.3 reshape.606
  454.0 10.4 all-reduce.22
  473.8 2.9 copy.210
  479.5 3.1 copy.212
  482.6 4.1 fusion.159
  489.2 210.1 %all-gather.9.cloned.1.call-done = f32[64,16,64,128]{3,2,1,0:T(8,128)} async-done(((f32[2,16,64,128]{3,2,1,0:T(8,128)}), f32[64,16,64,128]{3,2,1,0:T(8,128)}) %all-gather.9.cloned.1.call-update) | async-done | bytes 33554448 | tf_op jit(solution)/shard_map/all_gather | solution.py:23
  699.3 23.3 %rev.7 = f32[32,2,16,64,128]{4,3,2,1,0:T(8,128)} reverse(f32[32,2,16,64,128]{4,3,2,1,0:T(8,128)} %bitcast.608), dimensions={0} | reverse | bytes 67108864 | tf_op jit(solution)/shard_map/rev | solution.py:25
  722.6 46.6 %while.163 = (s32[]{:T(128)}, f32[2,16,64,128]{3,2,1,0:T(8,128)S(1)}, s32[]{:T(128)}, f32[32,2,16]{2,1,0:T(2,128)S(1)}, f32[32,2,16,64,128]{4,3,2,1,0:T(8,128)}, /*index=5*/s32[]{:T(128)}, s32[]{:T(128)}) while((s32[]{:T(128)}, f32[2,16,64,128]{3,2,1,0:T(8,128)S(1)}, s32[]{:T(128)}, f32[32,2,16]{2,1,0:T(2,128)S(1)}, ...), condition=%wide.region_23.24_spmd.clone, body=%wide.region_22.23_spmd.clone.sunk | while | flops 1048580 | bytes 3146225 | solution.py:35
  772.7 91.6 %while.164 = (s32[]{:T(128)}, f32[2,16]{1,0:T(2,128)}, f32[2,16,64,128]{3,2,1,0:T(8,128)S(1)}, bf16[2,128,2,16,64]{1,4,3,2,0:T(8,128)(2,1)}, bf16[2,128,2,128]{3...) while((s32[]{:T(128)}, f32[2,16]{1,0:T(2,128)}, ...), condition=%wide.region_35.36_spmd.clone, body=%wide.region_24.35_spmd.clone.sunk | while | flops 431345728 | bytes 55708368 | solution.py:114
  780.7 5.2 fusion.275
  799.4 3.2 reduce_window_sum.95
  826.5 5.2 fusion.275
  845.2 3.2 reduce_window_sum.95
  867.9 4.3 multiply_reduce_fusion.3
  881.2 5.1 collective-permute-start.2
  887.6 3.1 collective-permute-start.3
  899.3 274.8 %all-reduce.21 = (f32[4,2048]{1,0:T(4,128)S(1)}, f32[2048]{0:T(1024)}, f32[4,2,256]{2,1,0:T(2,128)S(1)}, f32[2,256]{1,0:T(2,128)}, f32[32]{0:T(128)}, /*index=5*/f32[32]{0:T(128)}, f32[32]{0:T(128)}, f32[2048]{0:T(1024)}) all-reduce(f32[4,2048]{1,0:T(4,128)S(1)} %pad_add_fusion.4, ...), channel_id=1, replica_groups=mesh['dp'=2,'ctx'=32,'head'=4] {'dp','ctx'}, use_global_device_ids=true, to_apply=%region_40.41 | all-reduce | flops 14944 | bytes 119552 | tf_op jit(solution)/shard_map/psum | solution.py:288
  (772 shorter events, 321.8 us)
Async XLA Ops:
  7.2 21.0 %copy-start.120 = (f32[2,256]{1,0:T(2,128)S(1)}, f32[2,256]{1,0:T(2,128)}, u32[]{:S(2)}) copy-start(f32[2,256]{1,0:T(2,128)} %param.36) | copy-start | bytes 6148
  7.2 278.0 %all-gather.7.cloned.1.call-start = ((), (), s32[]{:S(2)}) async-start(), calls=%async_computation | async-start | bytes 34603008 | tf_op jit(solution)/shard_map/all_gather | solution.py:23
  12.5 17.1 %collective-permute-start = (bf16[3,2048]{1,0:T(4,128)(2,1)S(1)}, bf16[3,2048]{1,0:T(4,128)(2,1)S(1)}, u32[]{:S(2)}, u32[]{:S(2)}) collective-permute-start(bf16[3,2048]{1,0:T(4,128)(2,1)S(1)} %bitcast_multiply_fusion.16), channel_id=1, source_target_pairs={{0,4},{4,8},{8,12},{12,16},{16,20},{20,24},{24,28},{28,32},{32,36}... | collective-permute-start | bytes 36872 | tf_op jit(solution)/shard_map/ppermute | solution.py:18
  17.0 10.2 collective-permute-start.1
  20.6 8.8 copy-start.86
  20.6 8.8 copy-start.90
  20.6 8.8 copy-start.94
  23.0 6.3 copy-start.48
  53.7 645.6 %all-gather.9.cloned.1.call-start = ((), (), s32[]{:S(2)}) async-start(), calls=%async_computation.1 | async-start | bytes 34603008 | tf_op jit(solution)/shard_map/all_gather | solution.py:23
  376.9 6.4 copy-start.57
  376.9 6.4 copy-start.71
  376.9 6.4 copy-start.75
  376.9 7.3 copy-start.73
  376.9 7.9 copy-start.64
  376.9 7.9 copy-start.66
  394.7 6.3 copy-start.35
  432.2 6.4 copy-start.57
  432.2 6.5 copy-start.71
  432.2 6.5 copy-start.75
  432.2 7.3 copy-start.73
  432.2 7.9 copy-start.64
  432.2 7.9 copy-start.66
  453.1 11.4 copy-start.14
  880.8 10.7 copy-start.49
  880.8 10.7 copy-start.50
  880.8 10.7 copy-start.118
  881.2 12.0 %copy-start.85 = (bf16[1,32,256]{2,1,0:T(8,128)(2,1)S(1)}, bf16[1,32,256]{2,1,0:T(8,128)(2,1)}, u32[]{:S(2)}) copy-start(bf16[1,32,256]{2,1,0:T(8,128)(2,1)} %param.31) | copy-start | bytes 49156
  881.2 300.9 %collective-permute-start.2 = (f32[3,2048]{1,0:T(4,128)S(1)}, f32[3,2048]{1,0:T(4,128)S(1)}, u32[]{:S(2)}, u32[]{:S(2)}) collective-permute-start(f32[3,2048]{1,0:T(4,128)S(1)} %copy-done.101), channel_id=1, source_target_pairs={{4,0},{8,4},{12,8},{16,12},{20,16},{24,20},{28,24},{32,28},{36,32}... | collective-permute-start | bytes 73736 | tf_op jit(solution)/shard_map/ppermute | solution.py:18
  887.6 292.6 %collective-permute-start.3 = (f32[3,2,256]{2,0,1:T(4,128)}, f32[3,2,256]{2,0,1:T(4,128)}, u32[]{:S(2)}, u32[]{:S(2)}) collective-permute-start(f32[3,2,256]{2,0,1:T(4,128)} %pad_add_fusion.5), channel_id=1, source_target_pairs={{4,0},{8,4},{12,8},{16,12},{20,16},{24,20},{28,24},{32,28},{36,32}... | collective-permute-start | bytes 18440 | tf_op jit(solution)/shard_map/ppermute | solution.py:18
  893.2 287.9 %copy-start.55 = (bf16[1,253,2,256]{3,1,2,0:T(8,128)(2,1)S(1)}, bf16[1,253,2,256]{3,1,2,0:T(8,128)(2,1)}, u32[]{:S(2)}) copy-start(bf16[1,253,2,256]{3,1,2,0:T(8,128)(2,1)} %fusion.164) | copy-start | bytes 777220
  1174.0 8.0 copy-start.9
  1174.1 8.0 copy-start.116
  (145 other events, 415.4 us)
Sparse Core Ops, SparseCore 0:
  53.8 231.3 all-gather.6
  471.0 228.2 all-gather.8
where the time goes:
time: 1200 us; the launch traced here: 1190 us
  waiting for transfers between devices  379 us (32%)
  blocking collectives  327 us (27%)
  other arithmetic  217 us (18%)
  local copies, waits for them, and re-layouts  198 us (16%)
  matrix products  32.7 us (3%)
  starting transfers between devices  15.2 us (1%)
  between operations  15 us (1%)
    all_gather x2, waiting for transfers between devices, entering(): pieces = jax.tree.map(lambda part: lax.all_gather(part, axis), value)  379 us
    psum x1, blocking collectives, per_device(): lax.psum((local_terms[0], local_terms[1], local_terms[2], local_terms[3],...  275 us
    select_n x62, other arithmetic, step(): jnp.where(position < mine, new, old)  90.6 us
    dynamic_update_slice x20, local copies, waits for them, and re-layouts, scan_blocks(): final_state, outputs = lax.scan(stepper, state_in, pieces)  65.8 us
    all_gather x1, blocking collectives, entering(): pieces = jax.tree.map(lambda part: lax.all_gather(part, axis), value)  41.9 us
  transfers between devices with their start and end apart: 6, of which 2 were waited for; matrix products, arithmetic and copies ran while one was open for 5% of the time, Pallas kernels for 0%

commit v1 on v0

--- a/solution.py
+++ b/solution.py
@@ -286,17 +286,20 @@
     )
     local_terms = (d_cxw, d_cxb, d_cbw, d_cbb, d_alog, d_dt_bias, d_skip, gain_local)
     summed_terms = lax.psum(
-        (
-            local_terms[0],
-            local_terms[1],
-            local_terms[2],
-            local_terms[3],
-            local_terms[4],
-            local_terms[5],
-            local_terms[6],
-            local_terms[7],
+        lax.psum(
+            (
+                local_terms[0],
+                local_terms[1],
+                local_terms[2],
+                local_terms[3],
+                local_terms[4],
+                local_terms[5],
+                local_terms[6],
+                local_terms[7],
+            ),
+            "dp",
         ),
-        ("dp", "ctx"),
+        "ctx",
     )
     grad_scale = float(lax.axis_size("dp") * lax.axis_size("ctx") * row_count) ** (-0.5)
     return (

time: 1200 us -> 1070 us (0.89)
  blocking collectives: 327 us -> 196 us
    psum x1, blocking collectives: 275 us -> 4.77 us  [per_device(): lax.psum((local_terms[0], local_terms[1], local_terms[2], local_terms[3],...]
    psum x0 -> x1, blocking collectives: none -> 139 us  [per_device(): lax.psum(lax.psum((local_terms[0], local_terms[1], local_terms[2], local_...]
  transfers between devices with their start and end apart: 6 -> 6, of which waited for: 2 -> 2; matrix products, arithmetic and copies ran while one was open for 5% -> 6% of each run, Pallas kernels for 0% -> 0%
where the time goes in v1:
time: 1070 us; the launch traced here: 1060 us
  waiting for transfers between devices  379 us (35%)
  other arithmetic  217 us (20%)
  local copies, waits for them, and re-layouts  198 us (19%)
  blocking collectives  196 us (18%)
  matrix products  32.6 us (3%)
  starting transfers between devices  15.2 us (1%)
  between operations  15 us (1%)
    all_gather x2, waiting for transfers between devices, entering(): pieces = jax.tree.map(lambda part: lax.all_gather(part, axis), value)  379 us
    psum x1, blocking collectives, per_device(): lax.psum(lax.psum((local_terms[0], local_terms[1], local_terms[2], local_...  139 us
    select_n x62, other arithmetic, step(): jnp.where(position < mine, new, old)  90.6 us
    dynamic_update_slice x20, local copies, waits for them, and re-layouts, scan_blocks(): final_state, outputs = lax.scan(stepper, state_in, pieces)  66 us
    all_gather x1, blocking collectives, entering(): pieces = jax.tree.map(lambda part: lax.all_gather(part, axis), value)  41.9 us
    rev x2, local copies, waits for them, and re-layouts, entering(): pieces = jax.tree.map(lambda part: part[::-1], pieces)  23.3 us
    dynamic_update_slice x18, other arithmetic, scan_blocks(): final_state, outputs = lax.scan(stepper, state_in, pieces)  22.7 us
  transfers between devices with their start and end apart: 6, of which 2 were waited for; matrix products, arithmetic and copies ran while one was open for 6% of the time, Pallas kernels for 0%

profile of v1, /device:TPU:128, one launch (start us, length us, event | category | flops | bytes accessed | tf_op | source)
XLA Modules:
  0.0 1059.3 jit_solution(10359379535267064781)
XLA Ops:
  12.5 3.5 collective-permute-start
  17.0 3.5 collective-permute-start.1
  30.2 3.8 multiply_convert_fusion.7
  34.9 3.1 reshape.652
  38.0 3.3 copy.180
  41.4 11.3 %while.160 = (s32[]{:T(128)}, f32[2,16]{1,0:T(2,128)S(1)}, f32[2,16,64,128]{3,2,1,0:T(8,128)S(1)}, f32[2,128]{1,0:T(2,128)}, f32[2,16,1]{1,0,2:T(2,128)}, /*inde...) while((s32[]{:T(128)}, f32[2,16]{1,0:T(2,128)S(1)}, ...), condition=%wide.region_5.6_spmd.clone, body=%wide.region_2.5_spmd.clone.sunk | while | flops 69234784 | bytes 2825641 | solution.py:139
  61.6 9.9 while.158
  74.2 41.9 %all-gather.3 = f32[32,2,16]{2,1,0:T(2,128)S(1)} all-gather(f32[1,2,16]{2,1,0:T(2,128)S(1)} %bitcast.631), channel_id=2, replica_groups=mesh['dp'=2,'ctx'=32,'head'=4] {'ctx'}, dimensions={0}, use_global_device_ids=true | all-gather | bytes 4224 | tf_op jit(solution)/shard_map/all_gather | solution.py:23
  116.1 169.0 %all-gather.7.cloned.1.call-done = f32[64,16,64,128]{3,2,1,0:T(8,128)} async-done(((f32[2,16,64,128]{3,2,1,0:T(8,128)}), f32[64,16,64,128]{3,2,1,0:T(8,128)}) %all-gather.7.cloned.1.call-update) | async-done | bytes 33554448 | tf_op jit(solution)/shard_map/all_gather | solution.py:23
  285.1 46.6 %while.161 = (s32[]{:T(128)}, f32[2,16,64,128]{3,2,1,0:T(8,128)S(1)}, s32[]{:T(128)}, f32[32,2,16]{2,1,0:T(2,128)S(1)}, f32[32,2,16,64,128]{4,3,2,1,0:T(8,128)}, /*index=5*/s32[]{:T(128)}, s32[]{:T(128)}) while((s32[]{:T(128)}, f32[2,16,64,128]{3,2,1,0:T(8,128)S(1)}, s32[]{:T(128)}, f32[32,2,16]{2,1,0:T(2,128)S(1)}, ...), condition=%wide.region_7.8_spmd.clone, body=%wide.region_6.7_spmd.clone.sunk | while | flops 1048580 | bytes 3146225 | solution.py:35
  334.8 110.8 %while.159 = (s32[]{:T(128)}, f32[2,16,64,128]{3,2,1,0:T(8,128)S(1)}, f32[2,128,2,16,64]{1,0,4,3,2:T(2,128)}, pred[2,2,16,128,128]{4,3,2,1,0:T(32,128)(4,1)}, f3...) while((s32[]{:T(128)}, ...), condition=%wide.region_11.12_spmd.clone, body=%wide.region_8.11_spmd.clone.sunk | while | flops 222142656 | bytes 67194320 | solution.py:114
  350.2 25.0 %dynamic_update_slice.324 = f32[2,128,2,16,64]{1,0,4,3,2:T(2,128)} dynamic-update-slice(f32[2,128,2,16,64]{1,0,4,3,2:T(2,128)} %get-tuple-element.3491, f32[1,128,2,16,64]{1,0,4,3,2:T(1,128)} %bitcast.609, s32[]{:T(128)S(6)} %copy.383, s32[]{:T(128)} %constant.352.clone.1..sunk, s32[]{:T(128)} %constant.352.clone.1..sunk, s32[]{:T(128)} %constant.352.clone.1..sunk, s32[]{:T(128)} %constant.352.clone.1..sunk) | dynamic-update-slice | bytes 2097156 | tf_op jit(solution)/shard_map/jvp()/while/body/jit(dynamic_update_index_in_dim)/dynamic_update_slice | solution.py:114
  377.0 4.0 fusion.249
  405.6 25.0 %dynamic_update_slice.324 = f32[2,128,2,16,64]{1,0,4,3,2:T(2,128)} dynamic-update-slice(f32[2,128,2,16,64]{1,0,4,3,2:T(2,128)} %get-tuple-element.3491, f32[1,128,2,16,64]{1,0,4,3,2:T(1,128)} %bitcast.609, s32[]{:T(128)S(6)} %copy.383, s32[]{:T(128)} %constant.352.clone.1..sunk, s32[]{:T(128)} %constant.352.clone.1..sunk, s32[]{:T(128)} %constant.352.clone.1..sunk, s32[]{:T(128)} %constant.352.clone.1..sunk) | dynamic-update-slice | bytes 2097156 | tf_op jit(solution)/shard_map/jvp()/while/body/jit(dynamic_update_index_in_dim)/dynamic_update_slice | solution.py:114
  432.4 4.0 fusion.249
  445.6 4.3 reshape.606
  454.4 10.4 all-reduce.22
  479.8 3.1 copy.212
  482.9 4.1 fusion.159
  489.4 210.2 %all-gather.9.cloned.1.call-done = f32[64,16,64,128]{3,2,1,0:T(8,128)} async-done(((f32[2,16,64,128]{3,2,1,0:T(8,128)}), f32[64,16,64,128]{3,2,1,0:T(8,128)}) %all-gather.9.cloned.1.call-update) | async-done | bytes 33554448 | tf_op jit(solution)/shard_map/all_gather | solution.py:23
  699.6 23.3 %rev.7 = f32[32,2,16,64,128]{4,3,2,1,0:T(8,128)} reverse(f32[32,2,16,64,128]{4,3,2,1,0:T(8,128)} %bitcast.608), dimensions={0} | reverse | bytes 67108864 | tf_op jit(solution)/shard_map/rev | solution.py:25
  722.9 46.6 %while.163 = (s32[]{:T(128)}, f32[2,16,64,128]{3,2,1,0:T(8,128)S(1)}, s32[]{:T(128)}, f32[32,2,16]{2,1,0:T(2,128)S(1)}, f32[32,2,16,64,128]{4,3,2,1,0:T(8,128)}, /*index=5*/s32[]{:T(128)}, s32[]{:T(128)}) while((s32[]{:T(128)}, f32[2,16,64,128]{3,2,1,0:T(8,128)S(1)}, s32[]{:T(128)}, f32[32,2,16]{2,1,0:T(2,128)S(1)}, ...), condition=%wide.region_23.24_spmd.clone, body=%wide.region_22.23_spmd.clone.sunk | while | flops 1048580 | bytes 3146225 | solution.py:35
  773.0 91.9 %while.164 = (s32[]{:T(128)}, f32[2,16]{1,0:T(2,128)}, f32[2,16,64,128]{3,2,1,0:T(8,128)S(1)}, bf16[2,128,2,16,64]{1,4,3,2,0:T(8,128)(2,1)}, bf16[2,128,2,128]{3...) while((s32[]{:T(128)}, f32[2,16]{1,0:T(2,128)}, ...), condition=%wide.region_35.36_spmd.clone, body=%wide.region_24.35_spmd.clone.sunk | while | flops 431345728 | bytes 55708368 | solution.py:114
  781.0 5.2 fusion.275
  799.6 3.2 reduce_window_sum.95
  826.9 5.2 fusion.275
  845.6 3.2 reduce_window_sum.95
  868.5 4.3 multiply_reduce_fusion.3
  881.7 5.1 collective-permute-start.2
  888.2 3.1 collective-permute-start.3
  898.8 4.8 all-reduce.23
  903.6 138.6 %all-reduce.21 = (f32[4,2048]{1,0:T(4,128)S(1)}, f32[2048]{0:T(1024)S(1)}, f32[4,2,256]{2,1,0:T(2,128)S(1)}, f32[2,256]{1,0:T(2,128)}, f32[32]{0:T(128)}, /*index=5*/f32[32]{0:T(128)}, f32[32]{0:T(128)}, f32[2048]{0:T(1024)}) all-reduce(f32[4,2048]{1,0:T(4,128)S(1)} %get-tuple-element.2662, ...), channel_id=1, replica_groups=mesh['dp'=2,'ctx'=32,'head'=4] {'ctx'}, use_global_device_ids=true, to_apply=%region_41.42 | all-reduce | flops 14944 | bytes 119552 | tf_op jit(solution)/shard_map/psum | solution.py:288
  (773 shorter events, 324.0 us)
Async XLA Ops:
  7.2 20.9 %copy-start.120 = (f32[2,256]{1,0:T(2,128)S(1)}, f32[2,256]{1,0:T(2,128)}, u32[]{:S(2)}) copy-start(f32[2,256]{1,0:T(2,128)} %param.36) | copy-start | bytes 6148
  7.2 278.0 %all-gather.7.cloned.1.call-start = ((), (), s32[]{:S(2)}) async-start(), calls=%async_computation | async-start | bytes 34603008 | tf_op jit(solution)/shard_map/all_gather | solution.py:23
  12.5 17.1 %collective-permute-start = (bf16[3,2048]{1,0:T(4,128)(2,1)S(1)}, bf16[3,2048]{1,0:T(4,128)(2,1)S(1)}, u32[]{:S(2)}, u32[]{:S(2)}) collective-permute-start(bf16[3,2048]{1,0:T(4,128)(2,1)S(1)} %bitcast_multiply_fusion.16), channel_id=1, source_target_pairs={{0,4},{4,8},{8,12},{12,16},{16,20},{20,24},{24,28},{28,32},{32,36}... | collective-permute-start | bytes 36872 | tf_op jit(solution)/shard_map/ppermute | solution.py:18
  17.0 10.2 collective-permute-start.1
  20.6 8.8 copy-start.86
  20.6 8.8 copy-start.90
  20.6 8.8 copy-start.94
  23.0 6.3 copy-start.48
  53.7 646.0 %all-gather.9.cloned.1.call-start = ((), (), s32[]{:S(2)}) async-start(), calls=%async_computation.1 | async-start | bytes 34603008 | tf_op jit(solution)/shard_map/all_gather | solution.py:23
  339.5 6.3 copy-start.35
  376.9 6.4 copy-start.57
  376.9 6.4 copy-start.71
  376.9 6.4 copy-start.75
  377.0 7.3 copy-start.73
  377.0 7.9 copy-start.64
  377.0 7.9 copy-start.66
  432.3 6.5 copy-start.57
  432.3 6.5 copy-start.71
  432.3 6.5 copy-start.75
  432.3 7.3 copy-start.73
  432.4 7.9 copy-start.64
  432.4 7.9 copy-start.66
  453.4 11.4 %copy-start.14 = (f32[1,256,2048]{1,2,0:T(8,128)S(1)}, f32[1,256,2048]{1,2,0:T(8,128)}, u32[]{:S(2)}) copy-start(f32[1,256,2048]{1,2,0:T(8,128)} %copy.183) | copy-start | bytes 6291460
  881.3 10.7 %copy-start.49 = (f32[2,16,2,128]{1,0,3,2:T(2,128)S(1)}, f32[2,16,2,128]{1,0,3,2:T(2,128)}, u32[]{:S(2)}) copy-start(f32[2,16,2,128]{1,0,3,2:T(2,128)} %copy-done.48) | copy-start | bytes 98308
  881.3 10.7 %copy-start.50 = (f32[2,2,16,128]{2,1,3,0:T(2,128)S(1)}, f32[2,2,16,128]{2,1,3,0:T(2,128)}, u32[]{:S(2)}) copy-start(f32[2,2,16,128]{2,1,3,0:T(2,128)} %get-tuple-element.1723) | copy-start | bytes 98308
  881.3 10.7 %copy-start.118 = (f32[2,16]{1,0:T(2,128)S(1)}, f32[2,16]{1,0:T(2,128)}, u32[]{:S(2)}) copy-start(f32[2,16]{1,0:T(2,128)} %copy-done.117) | copy-start | bytes 388
  881.7 12.0 %copy-start.85 = (bf16[1,32,256]{2,1,0:T(8,128)(2,1)S(1)}, bf16[1,32,256]{2,1,0:T(8,128)(2,1)}, u32[]{:S(2)}) copy-start(bf16[1,32,256]{2,1,0:T(8,128)(2,1)} %param.31) | copy-start | bytes 49156
  881.7 168.4 %collective-permute-start.2 = (f32[3,2048]{1,0:T(4,128)S(1)}, f32[3,2048]{1,0:T(4,128)S(1)}, u32[]{:S(2)}, u32[]{:S(2)}) collective-permute-start(f32[3,2048]{1,0:T(4,128)S(1)} %copy-done.101), channel_id=1, source_target_pairs={{4,0},{8,4},{12,8},{16,12},{20,16},{24,20},{28,24},{32,28},{36,32}... | collective-permute-start | bytes 73736 | tf_op jit(solution)/shard_map/ppermute | solution.py:18
  888.2 160.1 %collective-permute-start.3 = (f32[3,2,256]{2,0,1:T(4,128)}, f32[3,2,256]{2,0,1:T(4,128)}, u32[]{:S(2)}, u32[]{:S(2)}) collective-permute-start(f32[3,2,256]{2,0,1:T(4,128)} %pad_add_fusion.5), channel_id=1, source_target_pairs={{4,0},{8,4},{12,8},{16,12},{20,16},{24,20},{28,24},{32,28},{36,32}... | collective-permute-start | bytes 18440 | tf_op jit(solution)/shard_map/ppermute | solution.py:18
  893.7 155.4 %copy-start.55 = (bf16[1,253,2,256]{3,1,2,0:T(8,128)(2,1)S(1)}, bf16[1,253,2,256]{3,1,2,0:T(8,128)(2,1)}, u32[]{:S(2)}) copy-start(bf16[1,253,2,256]{3,1,2,0:T(8,128)(2,1)} %fusion.164) | copy-start | bytes 777220
  1042.2 8.0 copy-start.9
  1042.2 8.0 copy-start.116
  (145 other events, 416.4 us)
Sparse Core Ops, SparseCore 0:
  53.8 231.3 all-gather.6
  471.3 228.2 all-gather.8
